TPU v7x, 512 devices: a whole 4x8x8 slice. The times are simulated.
512 devices in a mesh: gx: 16 (over y, core), gy: 32 (over z, x).
Axes of the slice: x: 4, y: 8, z: 8, core: 2. Of those that a mesh axis runs over, the one named last changes fastest.
Arguments:
- inputs: bfloat16 [256, 4, 2304], P('gy', None, 'gx'), may hold values from -8 to 8
- cache_pool: bfloat16 [2, 64, 4096, 1024], P(None, 'gx', 'gy'), may hold values from -6 to 6
- lengths: int32 [32], P('gy'), may hold values from 1 to 32768, as said below
- block_table: int32 [32, 33], P('gy'), may hold values from -1 to 63, as said below
- parents: int32 [3, 256], P(None, 'gy'), may hold values from 0 to 7
- norm_gains: float32 [4, 2304], P(None, 'gx'), may hold values from -0.5 to 1
- w_query: bfloat16 [2304, 2048], P('gx', 'gy'), may hold values from -0.125 to 0.125
- w_key: bfloat16 [2304, 1024], P('gx', 'gy'), may hold values from -0.125 to 0.125
- w_value: bfloat16 [2304, 1024], P('gx', 'gy'), may hold values from -0.125 to 0.125
- w_out: bfloat16 [2048, 2304], P('gy', 'gx'), may hold values from -1 to 1
- w_gate: bfloat16 [2304, 9216], P('gx', 'gy'), may hold values from -0.125 to 0.125
- w_up: bfloat16 [2304, 9216], P('gx', 'gy'), may hold values from -0.125 to 0.125
- w_down: bfloat16 [9216, 2304], P('gy', 'gx'), may hold values from -1 to 1
Outputs:
- outputs: bfloat16 [256, 4, 2304], P('gy', None, 'gx')
Inputs may be any that keep to these rules, and one draw needn't show every extreme that they name: `lengths`: a group's beams share its prompt length. block_table[g, j] is the slot, numbered over the index of gy that holds group g as gx index times 4 plus the device's slot, of page first(g) + j of the group, for j up to (lengths[g] - 1) // 128 - first(g), and -1 beyond; no slot is named twice; a device holds at most 4 pages, and some device holds 4. Beam b at step s + 1 continues beam parents[s, b] of its own group, numbered within the group.
All inputs are finite; a program needn't handle non-finite values.
Results may differ from a plain program's by a relative error of at most 0.015.
Values may be sent and summed in bfloat16 or wider, within the bound.
A program may use at most 64 MiB of HBM per device.

v0:
```python
import jax
import jax.numpy as jnp
from jax import lax
from jax.sharding import PartitionSpec as P

D = 2304
HEADS = 8
KV_HEADS = 4
HEAD_DIM = 256
WINDOW = 4096
PAGE = 128
BEAM = 8
EPSILON = 1e-06
SOFT_CAP = 50.0
ROPE_BASE = 10000.0


def rotate(values, positions):
    half_width = values.shape[-1] // 2
    inverse_freq = ROPE_BASE ** (
        -jnp.arange(half_width, dtype=jnp.float32) * 2.0 / values.shape[-1]
    )
    angles = positions[..., None].astype(jnp.float32) * inverse_freq
    cosine = jnp.cos(angles)[..., None, :]
    sine_part = jnp.sin(angles)[..., None, :]
    first_half = values[..., :half_width]
    second_half = values[..., half_width:]
    return jnp.concatenate(
        [
            first_half * cosine - second_half * sine_part,
            second_half * cosine + first_half * sine_part,
        ],
        axis=-1,
    )


def ancestry(parents, beam_count, group_size, steps_count):
    beam_ids = jnp.arange(beam_count, dtype=jnp.int32)
    group_base = beam_ids // group_size * group_size
    table_rows = []
    for moment in range(steps_count):
        current = beam_ids
        chain_list = [beam_ids] * steps_count
        for earlier in range(moment, 0, -1):
            current = group_base + jnp.take(parents[earlier - 1], current)
            chain_list[earlier - 1] = current
        table_rows.append(jnp.stack(chain_list))
    return jnp.stack(table_rows)


def tail_terms(grouped, key_steps, value_steps, ancestors):
    steps_count = grouped.shape[1]
    step_ids = jnp.arange(steps_count, dtype=jnp.int32)
    tail_keys = key_steps[ancestors, step_ids[None, :, None]]
    tail_values = value_steps[ancestors, step_ids[None, :, None]]
    scores = jnp.einsum(
        "bskgd,sjbkd->bskgj", grouped, tail_keys, preferred_element_type=jnp.float32
    )
    allowed = step_ids[None, :] <= step_ids[:, None]
    weights = jnp.where(
        allowed[None, :, None, None, :], jnp.exp(SOFT_CAP * jnp.tanh(scores / SOFT_CAP)), 0.0
    )
    numerator = jnp.einsum(
        "bskgj,sjbkd->bskgd",
        weights.astype(jnp.bfloat16),
        tail_values,
        preferred_element_type=jnp.float32,
    )
    return (numerator, jnp.sum(weights, axis=-1))


def body(
    inputs,
    cache_pool,
    lengths,
    block_table,
    parents,
    norm_gains,
    w_query,
    w_key,
    w_value,
    w_out,
    w_gate,
    w_up,
    w_down,
):
    col_beams, steps_count, width_part = inputs.shape
    group_count = lengths.shape[0]
    slot_count = cache_pool.shape[1]
    rep_heads = HEADS // KV_HEADS
    x_wide = inputs.astype(jnp.float32)
    gain_rows = 1.0 + norm_gains
    square_sum = lax.psum(jnp.sum(x_wide * x_wide, axis=-1), "gx")
    normed_share = (x_wide * lax.rsqrt(square_sum / D + EPSILON)[..., None] * gain_rows[0]).astype(
        jnp.bfloat16
    )
    normed = lax.all_gather(normed_share, "gy", axis=0, tiled=True)
    all_beams = normed.shape[0]
    flat_rows = normed.reshape(-1, width_part)

    def project(weight):
        return jnp.dot(flat_rows, weight, preferred_element_type=jnp.float32).reshape(
            all_beams, steps_count, weight.shape[1]
        )

    query_sum, key_sum, value_sum = lax.psum(
        (project(w_query), project(w_key), project(w_value)), "gx"
    )
    query_raw, key_raw, value_raw = (
        lax.all_to_all(query_sum, "gy", split_axis=0, concat_axis=2, tiled=True),
        lax.all_to_all(key_sum, "gy", split_axis=0, concat_axis=2, tiled=True),
        lax.all_to_all(value_sum, "gy", split_axis=0, concat_axis=2, tiled=True),
    )
    beam_lengths = jnp.repeat(lengths, BEAM)
    step_ids = jnp.arange(steps_count, dtype=jnp.int32)
    positions = beam_lengths[:, None] + step_ids[None, :]
    queries = (
        rotate(query_raw.reshape(col_beams, steps_count, HEADS, HEAD_DIM), positions)
        * HEAD_DIM ** (-0.5)
    ).astype(jnp.bfloat16)
    key_steps = rotate(
        key_raw.reshape(col_beams, steps_count, KV_HEADS, HEAD_DIM), positions
    ).astype(jnp.bfloat16)
    value_steps = value_raw.reshape(col_beams, steps_count, KV_HEADS, HEAD_DIM).astype(jnp.bfloat16)
    grouped = queries.reshape(col_beams, steps_count, KV_HEADS, rep_heads, HEAD_DIM)
    slot_ids = lax.axis_index("gx") * slot_count + jnp.arange(slot_count, dtype=jnp.int32)
    matches = block_table[:, :, None] == slot_ids[None, None, :]
    owner_mask = jnp.any(matches, axis=1)
    slot_used = jnp.any(owner_mask, axis=0)
    page_number = jnp.sum(
        jnp.where(matches, jnp.arange(block_table.shape[1], dtype=jnp.int32)[None, :, None], 0),
        axis=(0, 1),
    )
    first_page = jnp.maximum(lengths - WINDOW + 1, 0) // PAGE
    slot_first = jnp.sum(jnp.where(owner_mask, first_page[:, None], 0), axis=0)
    slot_length = jnp.sum(jnp.where(owner_mask, lengths[:, None], 0), axis=0)
    key_positions = (slot_first + page_number)[:, None] * PAGE + jnp.arange(PAGE, dtype=jnp.int32)[
        None, :
    ]
    group_queries = grouped.reshape(group_count, BEAM, steps_count, KV_HEADS, rep_heads, HEAD_DIM)
    slot_queries = jnp.einsum(
        "an,abskgd->nbskgd",
        owner_mask.astype(jnp.bfloat16),
        group_queries,
        preferred_element_type=jnp.float32,
    ).astype(jnp.bfloat16)
    page_keys = cache_pool[0].reshape(slot_count, PAGE, KV_HEADS, HEAD_DIM)
    page_values = cache_pool[1].reshape(slot_count, PAGE, KV_HEADS, HEAD_DIM)
    scores = jnp.einsum(
        "nbskgd,ntkd->nbskgt", slot_queries, page_keys, preferred_element_type=jnp.float32
    )
    lower_bound = slot_length[:, None] + step_ids[None, :] - WINDOW + 1
    visible = (
        slot_used[:, None, None]
        & (key_positions[:, None, :] < slot_length[:, None, None])
        & (key_positions[:, None, :] >= lower_bound[:, :, None])
    )
    weights = jnp.where(
        visible[:, None, :, None, None, :], jnp.exp(SOFT_CAP * jnp.tanh(scores / SOFT_CAP)), 0.0
    )
    page_den = jnp.sum(weights, axis=-1)
    page_num = jnp.einsum(
        "nbskgt,ntkd->nbskgd",
        weights.astype(jnp.bfloat16),
        page_values,
        preferred_element_type=jnp.float32,
    )
    owner_wide = owner_mask.astype(jnp.float32)
    group_num = jnp.sum(owner_wide[:, :, None, None, None, None, None] * page_num[None], axis=1)
    group_den = jnp.sum(owner_wide[:, :, None, None, None, None] * page_den[None], axis=1)
    total_num, total_den = lax.psum((group_num, group_den), "gx")
    ancestors = ancestry(parents, col_beams, BEAM, steps_count)
    tail_num, tail_den = tail_terms(grouped, key_steps, value_steps, ancestors)
    numerator = total_num.reshape(col_beams, steps_count, KV_HEADS, rep_heads, HEAD_DIM) + tail_num
    denominator = total_den.reshape(col_beams, steps_count, KV_HEADS, rep_heads) + tail_den
    attended = (
        (numerator / denominator[..., None])
        .astype(jnp.bfloat16)
        .reshape(col_beams, steps_count, HEADS * HEAD_DIM)
    )
    head_rows = lax.all_to_all(attended, "gy", split_axis=2, concat_axis=0, tiled=True)
    head_width = head_rows.shape[2]
    attn_part = jnp.dot(
        head_rows.reshape(-1, head_width), w_out, preferred_element_type=jnp.float32
    ).reshape(all_beams, steps_count, width_part)
    attn_full = lax.psum(attn_part, "gy")
    residual = lax.all_gather(inputs, "gy", axis=0, tiled=True).astype(jnp.float32)
    attn_square = lax.psum(jnp.sum(attn_full * attn_full, axis=-1), "gx")
    mixed_full = (
        residual + attn_full * lax.rsqrt(attn_square / D + EPSILON)[..., None] * gain_rows[1]
    )
    mixed_square = lax.psum(jnp.sum(mixed_full * mixed_full, axis=-1), "gx")
    ff_input = (
        mixed_full * lax.rsqrt(mixed_square / D + EPSILON)[..., None] * gain_rows[2]
    ).astype(jnp.bfloat16)
    mixed_rows = lax.dynamic_slice_in_dim(
        mixed_full, lax.axis_index("gy") * col_beams, col_beams, 0
    )
    gate_width = w_gate.shape[1]
    matrix_rows = ff_input.reshape(-1, width_part)
    gate_and_up = jnp.concatenate(
        [
            jnp.dot(matrix_rows, w_gate, preferred_element_type=jnp.float32),
            jnp.dot(matrix_rows, w_up, preferred_element_type=jnp.float32),
        ],
        axis=1,
    )
    activate_gate_and_up = lax.psum_scatter(
        gate_and_up.reshape(ff_input.shape[0], steps_count, 2 * gate_width),
        "gx",
        scatter_dimension=0,
        tiled=True,
    )
    hidden_share = (
        jax.nn.gelu(activate_gate_and_up[..., :gate_width], approximate=True)
        * activate_gate_and_up[..., gate_width:]
    ).astype(jnp.bfloat16)
    hidden_rows = lax.all_gather(hidden_share, "gx", axis=0, tiled=True)
    down_part = jnp.dot(
        hidden_rows.reshape(-1, gate_width), w_down, preferred_element_type=jnp.float32
    ).reshape(hidden_rows.shape[0], steps_count, width_part)
    down_own = lax.psum_scatter(down_part, "gy", scatter_dimension=0, tiled=True)
    out_square = lax.psum(jnp.sum(down_own * down_own, axis=-1), "gx")
    return (
        mixed_rows + down_own * lax.rsqrt(out_square / D + EPSILON)[..., None] * gain_rows[3]
    ).astype(jnp.bfloat16)


def solution(mesh):
    return jax.shard_map(
        body,
        mesh=mesh,
        in_specs=(
            P("gy", None, "gx"),
            P(None, "gx", "gy", None),
            P("gy"),
            P("gy", None),
            P(None, "gy"),
            P(None, "gx"),
            P("gx", "gy"),
            P("gx", "gy"),
            P("gx", "gy"),
            P("gy", "gx"),
            P("gx", "gy"),
            P("gx", "gy"),
            P("gy", "gx"),
        ),
        out_specs=P("gy", None, "gx"),
        check_vma=False,
    )
```

profile of v0, /device:TPU:1, one launch (start us, length us, event | category | flops | bytes accessed | tf_op | source)
XLA Modules:
  0.0 937.1 jit_solution(2836527621570253802)
XLA Ops:
  6.5 0.7 broadcast_add_fusion
  7.3 0.8 fusion.33
  8.1 29.8 %psum.70 = f32[8,4]{0,1:T(4,128)S(1)} all-reduce(f32[8,4]{0,1:T(4,128)S(1)} %fusion.33), channel_id=1, replica_groups=mesh['gx'=16,'gy'=32] {'gx'}, use_global_device_ids=true, to_apply=%region_3.0 | all-reduce | flops 32 | bytes 256 | tf_op jit(solution)/shard_map/psum | solution.py:93
  37.8 0.8 fusion.35
  38.6 36.1 %all_gather.10 = bf16[256,4,144]{2,0,1:T(8,128)(2,1)S(1)} all-gather(bf16[8,4,144]{2,0,1:T(8,128)(2,1)S(1)} %fusion.35), channel_id=1, replica_groups=mesh['gx'=16,'gy'=32] {'gy'}, dimensions={0}, use_global_device_ids=true | all-gather | bytes 304128 | tf_op jit(solution)/shard_map/all_gather | solution.py:97
  74.7 1.7 fusion.37
  76.5 0.8 compare_reduce_fusion
  77.4 0.8 fusion.49
  79.1 1.8 fusion.65
  80.9 0.6 gather_fusion.3
  81.6 0.6 gather_fusion.5
  82.2 0.6 gather_fusion.6
  82.9 0.6 gather_fusion.7
  83.6 0.6 gather_fusion.4
  84.6 111.0 %all-reduce.9.cloned.1.call-done = f32[256,4,64]{0,2,1:T(8,128)} async-done(((f32[256,4,64]{0,2,1:T(8,128)}), f32[256,4,64]{0,2,1:T(8,128)}) %all-reduce.9.cloned.1.call-update) | async-done | bytes 262160 | tf_op jit(solution)/shard_map/psum | solution.py:106
  195.6 1.2 copy.204
  196.8 1.2 reshape.614
  198.0 9.9 %all-to-all-start = ((f32[32,1,2048]{2,1,0:T(1,128)}), f32[32,1,2048]{2,1,0:T(1,128)S(1)}, u32[]{:S(2)}, u32[]{:S(2)}) async-start(f32[32,1,2048]{2,1,0:T(1,128)} %reshape.614), calls=%async_computation | async-start | bytes 524288 | tf_op jit(solution)/shard_map/all_to_all | solution.py:110
  207.9 0.6 gather_fusion.2
  208.5 1.3 copy.253
  209.9 0.7 copy.254
  210.7 0.9 fusion.44
  211.6 7.5 all-to-all-done
  219.6 1.3 reduce.5
  221.9 1.7 fusion.67
  224.1 0.8 copy.281
  225.1 47.4 %all-reduce.16 = (bf16[256,4,32]{0,2,1:T(8,128)(2,1)S(1)}, f32[8,4,4,2]{0,2,3,1:T(4,128)S(1)}) all-reduce(f32[256,4,32]{0,2,1:T(8,128)S(1)} %fusion.42, f32[8,4,4,2]{0,2,3,1:T(4,128)S(1)} %copy.223), channel_id=1, replica_groups=mesh['gx'=16,'gy'=32] {'gx'}, use_global_device_ids=true, to_apply=%region_8.10 | all-reduce | flops 33024 | bytes 198656 | tf_op jit(solution)/shard_map/psum | solution.py:106
  272.6 0.8 reshape.616
  273.5 3.8 all-to-all-start.2
  277.4 0.7 all-reduce.15.cloned.1.call-update
  278.1 120.2 %all-reduce.15.cloned.1.call-done = (f32[8,4,4,2,256]{4,3,2,1,0:T(2,128)}, f32[256,4,32]{0,2,1:T(8,128)}) async-done(((f32[8,4,4,2,256]{4,3,2,1,0:T(2,128)}, f32[256,4,32]{0,2,1:T(8,128)}), (f32[8,4,4,2,256]{4,3,2,1,0:T(2,128)}, f32[256,4,32]{0,2,1:T(8,128)})) %all-reduce.15.cloned.1.call-update) | async-done | bytes 393232 | tf_op jit(solution)/shard_map/psum | solution.py:171
  398.3 1.1 copy.213
  399.4 1.0 reshape.618
  400.4 9.9 %all-to-all-start.1 = ((f32[32,1,1024]{2,1,0:T(1,128)}), f32[32,1,1024]{2,1,0:T(1,128)S(1)}, u32[]{:S(2)}, u32[]{:S(2)}) async-start(f32[32,1,1024]{2,1,0:T(1,128)} %reshape.618), calls=%async_computation.1 | async-start | bytes 262144 | tf_op jit(solution)/shard_map/all_to_all | solution.py:111
  411.2 1.0 gather_fusion.1
  412.2 7.5 all-to-all-done.1
  419.7 1.0 reduce.6
  421.4 1.0 gather_fusion
  423.7 1.3 copy.250
  425.0 2.3 reshape.620
  427.3 12.7 %all_to_all.54 = bf16[32,2,1024]{2,1,0:T(2,128)(2,1)S(1)} all-to-all(bf16[32,2,1024]{2,1,0:T(2,128)(2,1)S(1)} %reshape.620), channel_id=1, replica_groups=mesh['gx'=16,'gy'=32] {'gy'}, dimensions={0} | all-to-all | bytes 262144 | tf_op jit(solution)/shard_map/all_to_all | solution.py:181
  440.0 2.4 reshape.621
  442.5 2.1 copy.252
  444.6 1.3 fusion.16
  446.0 37.6 %all_gather.9 = bf16[256,4,144]{2,1,0:T(4,128)(2,1)S(1)} all-gather(bf16[8,4,144]{2,1,0:T(4,128)(2,1)S(1)} %copy-done.2), channel_id=1, replica_groups=mesh['gx'=16,'gy'=32] {'gy'}, dimensions={0}, use_global_device_ids=true | all-gather | bytes 304128 | tf_op jit(solution)/shard_map/all_gather | solution.py:187
  483.6 115.7 %all-reduce.11.cloned.1.call-done = f32[256,4,144]{2,0,1:T(8,128)} async-done(((f32[256,4,144]{2,0,1:T(8,128)}), f32[256,4,144]{2,0,1:T(8,128)}) %all-reduce.11.cloned.1.call-update) | async-done | bytes 589840 | tf_op jit(solution)/shard_map/psum | solution.py:186
  599.3 1.4 multiply_reduce_fusion.1
  600.8 28.1 %psum.77 = f32[256,4]{0,1:T(4,128)S(1)} all-reduce(f32[256,4]{0,1:T(4,128)S(1)} %multiply_reduce_fusion.1), channel_id=1, replica_groups=mesh['gx'=16,'gy'=32] {'gx'}, use_global_device_ids=true, to_apply=%region_15.17 | all-reduce | flops 1024 | bytes 8192 | tf_op jit(solution)/shard_map/psum | solution.py:188
  628.9 1.6 multiply_reduce_fusion
  630.5 23.6 %psum.78 = f32[256,4]{0,1:T(4,128)S(1)} all-reduce(f32[256,4]{0,1:T(4,128)S(1)} %get-tuple-element.12), channel_id=1, replica_groups=mesh['gx'=16,'gy'=32] {'gx'}, use_global_device_ids=true, to_apply=%region_17.19 | all-reduce | flops 1024 | bytes 8192 | tf_op jit(solution)/shard_map/psum | solution.py:192
  655.9 1.6 pad_maximum_fusion
  657.4 2.1 copy.232
  659.5 1.9 reshape.525
  661.5 3.4 copy.233
  665.0 57.8 %reduce-scatter.2.cloned.1.call-done = f32[16,4,576]{2,0,1:T(8,128)} async-done(((f32[256,4,576]{2,0,1:T(8,128)}), f32[16,4,576]{2,0,1:T(8,128)}) %reduce-scatter.2.cloned.1.call-update) | async-done | bytes 147472 | tf_op jit(solution)/shard_map/reduce_scatter | solution.py:208
  722.8 1.1 fusion.31
  723.8 19.0 %all_gather.11 = bf16[256,4,288]{2,0,1:T(8,128)(2,1)S(1)} all-gather(bf16[16,4,288]{2,0,1:T(8,128)(2,1)S(1)} %fusion.31), channel_id=1, replica_groups=mesh['gx'=16,'gy'=32] {'gx'}, dimensions={0}, use_global_device_ids=true | all-gather | bytes 626688 | tf_op jit(solution)/shard_map/all_gather | solution.py:218
  743.3 1.7 copy.234
  745.0 1.3 dynamic-slice
  746.9 153.2 %all-reduce.13.cloned.1.call-done = f32[256,4,144]{2,1,0:T(4,128)} async-done(((f32[256,4,144]{2,1,0:T(4,128)}), f32[256,4,144]{2,1,0:T(4,128)}) %all-reduce.13.cloned.1.call-update) | async-done | bytes 589840
  900.1 0.8 multiply_reduce_fusion.3
  901.0 28.1 %psum.79 = f32[8,4]{0,1:T(4,128)S(1)} all-reduce(f32[8,4]{0,1:T(4,128)S(1)} %copy.235), channel_id=1, replica_groups=mesh['gx'=16,'gy'=32] {'gx'}, use_global_device_ids=true, to_apply=%region_21.23 | all-reduce | flops 32 | bytes 256 | tf_op jit(solution)/shard_map/psum | solution.py:223
  929.1 0.8 fusion.41
  930.0 0.6 copy.237
  (96 shorter events, 8.3 us)
Async XLA Ops:
  6.5 648.6 %copy-start = (bf16[144,288]{1,0:T(8,128)(2,1)S(1)}, bf16[144,288]{1,0:T(8,128)(2,1)}, u32[]{:S(2)}) copy-start(bf16[144,288]{1,0:T(8,128)(2,1)} %param.25) | copy-start | bytes 248836
  6.5 189.0 %all-reduce.9.cloned.1.call-start = ((), (), s32[]{:S(2)}) async-start(), calls=%async_computation.5 | async-start | bytes 524288 | tf_op jit(solution)/shard_map/psum | solution.py:106
  79.1 1.8 copy-start.8
  80.9 3.3 copy-start.6
  198.0 21.1 %all-to-all-start = ((f32[32,1,2048]{2,1,0:T(1,128)}), f32[32,1,2048]{2,1,0:T(1,128)S(1)}, u32[]{:S(2)}, u32[]{:S(2)}) async-start(f32[32,1,2048]{2,1,0:T(1,128)} %reshape.614), calls=%async_computation | async-start | bytes 524288 | tf_op jit(solution)/shard_map/all_to_all | solution.py:110
  208.5 2.1 copy-start.7
  273.5 126.9 %all-to-all-start.2 = ((bf16[32,2,512]{2,1,0:T(2,128)(2,1)}), bf16[32,2,512]{2,1,0:T(2,128)(2,1)S(1)}, u32[]{:S(2)}, u32[]{:S(2)}) async-start(bf16[32,2,512]{2,1,0:T(2,128)(2,1)} %reshape.616), calls=%async_computation.2 | async-start | bytes 131072 | tf_op jit(solution)/shard_map/all_to_all | solution.py:112
  277.3 121.0 %all-reduce.15.cloned.1.call-start = ((), (), s32[]{:S(2)}) async-start(), calls=%async_computation.9 | async-start | bytes 786432 | tf_op jit(solution)/shard_map/psum | solution.py:171
  400.4 19.3 %all-to-all-start.1 = ((f32[32,1,1024]{2,1,0:T(1,128)}), f32[32,1,1024]{2,1,0:T(1,128)S(1)}, u32[]{:S(2)}, u32[]{:S(2)}) async-start(f32[32,1,1024]{2,1,0:T(1,128)} %reshape.618), calls=%async_computation.1 | async-start | bytes 262144 | tf_op jit(solution)/shard_map/all_to_all | solution.py:111
  410.3 189.0 %all-reduce.11.cloned.1.call-start = ((), (), s32[]{:S(2)}) async-start(), calls=%async_computation.6 | async-start | bytes 2097152 | tf_op jit(solution)/shard_map/psum | solution.py:186
  421.3 2.0 copy-start.9
  440.0 4.6 copy-start.5
  442.5 3.5 copy-start.2
  445.9 276.8 %reduce-scatter.2.cloned.1.call-start = ((), (), s32[]{:S(2)}) async-start(), calls=%async_computation.7 | async-start | bytes 2785280 | tf_op jit(solution)/shard_map/reduce_scatter | solution.py:208
  630.5 23.8 %copy-start.1 = (f32[256,4,144]{2,0,1:T(8,128)}, f32[256,4,144]{2,0,1:T(8,128)S(1)}, u32[]{:S(2)}) copy-start(f32[256,4,144]{2,0,1:T(8,128)S(1)} %get-tuple-element.13) | copy-start | bytes 1769476
  654.3 1.1 copy-start.3
  664.9 77.9 %copy-start.4 = (bf16[288,144]{0,1:T(8,128)(2,1)S(1)}, bf16[288,144]{0,1:T(8,128)(2,1)}, u32[]{:S(2)}) copy-start(bf16[288,144]{0,1:T(8,128)(2,1)} %param.27) | copy-start | bytes 248836
  664.9 235.2 %all-reduce.13.cloned.1.call-start = ((), (), s32[]{:S(2)}) async-start(), calls=%async_computation.8 | async-start | bytes 2097152
Sparse Core Ops, SparseCore 0:
  76.6 118.8 all-reduce.8
  280.7 117.4 all-reduce.14
  446.0 153.2 all-reduce.10
  665.0 57.6 reduce-scatter.1
  745.1 154.9 all-reduce.12
where the time goes:
time: 938 us; the launch traced here: 937 us
  waiting for transfers between devices  574 us (61%)
  blocking collectives  262 us (28%)
  local copies, waits for them, and re-layouts  38.9 us (4%)
  starting transfers between devices  24 us (3%)
  between operations  15 us (2%)
  other arithmetic  14.8 us (2%)
    unnamed x6, waiting for transfers between devices  154 us
    psum x1, waiting for transfers between devices, body(): total_num, total_den = lax.psum((group_num, group_den), 'gx')  120 us
    psum x1, waiting for transfers between devices, body(): attn_full = lax.psum(attn_part, 'gy')  116 us
    psum x1, waiting for transfers between devices, body(): lax.psum((project(w_query), project(w_key), project(w_value)), 'gx')  111 us
    reduce_scatter x1, waiting for transfers between devices, body(): lax.psum_scatter(gate_and_up.reshape(ff_input.shape[0], steps_count, 2 *...  57.8 us
    psum x1, blocking collectives, body(): lax.psum((project(w_query), project(w_key), project(w_value)), 'gx')  47.4 us
    all_gather x1, blocking collectives, body(): lax.all_gather(inputs, 'gy', axis=0, tiled=True).astype(jnp.float32)  37.6 us
    all_gather x1, blocking collectives, body(): normed = lax.all_gather(normed_share, 'gy', axis=0, tiled=True)  36.1 us
  transfers between devices with their start and end apart: 8, of which 7 were waited for; matrix products, arithmetic and copies ran while one was open for 2% of the time, Pallas kernels for 0%

commit v1 on v0

--- a/solution.py
+++ b/solution.py
@@ -84,6 +84,14 @@
     w_up,
     w_down,
 ):
+
+    def search_weights(at_axis, mat, dim_no):
+        mat_out = lax.all_to_all(
+            jnp.stack(jnp.split(mat, lax.axis_size("gy"), axis=dim_no)), "gy", 0, 0
+        )
+        e_next = jnp.concatenate(mat_out, axis=at_axis)
+        return e_next
+
     col_beams, steps_count, width_part = inputs.shape
     group_count = lengths.shape[0]
     slot_count = cache_pool.shape[1]
@@ -107,7 +115,7 @@
         (project(w_query), project(w_key), project(w_value)), "gx"
     )
     query_raw, key_raw, value_raw = (
-        lax.all_to_all(query_sum, "gy", split_axis=0, concat_axis=2, tiled=True),
+        search_weights(2, mat=query_sum, dim_no=0),
         lax.all_to_all(key_sum, "gy", split_axis=0, concat_axis=2, tiled=True),
         lax.all_to_all(value_sum, "gy", split_axis=0, concat_axis=2, tiled=True),
     )

time: 938 us -> 971 us (1.035)
  local copies, waits for them, and re-layouts: 38.9 us -> 73.6 us
    another operation x1 -> x37, local copies, waits for them, and re-layouts: 0.16 us -> 29.8 us  [the longest x35 29.4 us: search_weights(): jnp.stack(jnp.split(mat, lax.axis_size('gy'), axis=dim_no))]
where the time goes in v1:
time: 971 us; the launch traced here: 969 us
  waiting for transfers between devices  568 us (58%)
  blocking collectives  262 us (27%)
  local copies, waits for them, and re-layouts  73.6 us (8%)
  starting transfers between devices  24 us (2%)
  other arithmetic  17.9 us (2%)
  between operations  15.4 us (2%)
    unnamed x6, waiting for transfers between devices  154 us
    psum x1, waiting for transfers between devices, body(): total_num, total_den = lax.psum((group_num, group_den), 'gx')  120 us
    psum x1, waiting for transfers between devices, body(): attn_full = lax.psum(attn_part, 'gy')  116 us
    psum x1, waiting for transfers between devices, body(): lax.psum((project(w_query), project(w_key), project(w_value)), 'gx')  106 us
    reduce_scatter x1, waiting for transfers between devices, body(): lax.psum_scatter(gate_and_up.reshape(ff_input.shape[0], steps_count, 2 *...  57.8 us
    psum x1, blocking collectives, body(): lax.psum((project(w_query), project(w_key), project(w_value)), 'gx')  47.3 us
    all_gather x1, blocking collectives, body(): lax.all_gather(inputs, 'gy', axis=0, tiled=True).astype(jnp.float32)  37.7 us
    all_gather x1, blocking collectives, body(): normed = lax.all_gather(normed_share, 'gy', axis=0, tiled=True)  36.1 us
  transfers between devices with their start and end apart: 8, of which 7 were waited for; matrix products, arithmetic and copies ran while one was open for 2% of the time, Pallas kernels for 0%

profile of v1, /device:TPU:1, one launch (start us, length us, event | category | flops | bytes accessed | tf_op | source)
XLA Modules:
  0.0 969.3 jit_solution(12792648736020877722)
XLA Ops:
  8.7 29.8 %psum.70 = f32[8,4]{0,1:T(4,128)S(1)} all-reduce(f32[8,4]{0,1:T(4,128)S(1)} %fusion.33), channel_id=1, replica_groups=mesh['gx'=16,'gy'=32] {'gx'}, use_global_device_ids=true, to_apply=%region_3.0 | all-reduce | flops 32 | bytes 256 | tf_op jit(solution)/shard_map/psum | solution.py:101
  39.2 36.1 %all_gather.10 = bf16[256,4,144]{2,0,1:T(8,128)(2,1)S(1)} all-gather(bf16[8,4,144]{2,0,1:T(8,128)(2,1)S(1)} %fusion.35), channel_id=1, replica_groups=mesh['gx'=16,'gy'=32] {'gy'}, dimensions={0}, use_global_device_ids=true | all-gather | bytes 304128 | tf_op jit(solution)/shard_map/all_gather | solution.py:105
  75.3 1.8 fusion.37
  80.2 2.8 fusion.65
  87.8 0.9 fusion.42
  89.9 106.2 %all-reduce.9.cloned.1.call-done = f32[256,4,64]{0,2,1:T(8,128)} async-done(((f32[256,4,64]{0,2,1:T(8,128)}), f32[256,4,64]{0,2,1:T(8,128)}) %all-reduce.9.cloned.1.call-update) | async-done | bytes 262160 | tf_op jit(solution)/shard_map/psum | solution.py:114
  196.2 3.4 slice_bitcast_fusion.19
  199.7 1.6 copy.323
  201.3 1.6 copy.324
  202.9 1.6 copy.325
  204.5 1.6 copy.326
  206.1 1.6 copy.327
  208.2 1.9 slice_bitcast_fusion
  210.1 1.6 copy.335
  211.8 1.6 copy.336
  213.3 1.6 copy.337
  214.9 1.6 copy.338
  216.5 1.6 copy.339
  218.1 1.0 copy.340
  219.1 1.0 copy.341
  220.1 1.0 copy.342
  221.1 1.0 copy.343
  222.1 1.0 copy.344
  223.1 1.0 copy.345
  224.0 1.0 copy.346
  229.6 1.0 reshape.613
  230.6 9.9 %all-to-all-start = ((f32[32,1,2048]{2,1,0:T(1,128)}), f32[32,1,2048]{2,1,0:T(1,128)S(1)}, u32[]{:S(2)}, u32[]{:S(2)}) async-start(f32[32,1,2048]{2,1,0:T(1,128)} %reshape.613), calls=%async_computation | async-start | bytes 524288 | tf_op jit(solution)/shard_map/all_to_all | solution.py:89
  241.2 2.3 copy.401
  244.2 0.9 fusion.44
  245.2 6.6 all-to-all-done
  252.2 1.3 reduce.5
  257.0 47.3 %all-reduce.16 = (bf16[256,4,32]{0,2,1:T(8,128)(2,1)S(1)}, f32[8,4,4,2]{0,2,3,1:T(4,128)S(1)}) all-reduce(f32[256,4,32]{0,2,1:T(8,128)S(1)} %copy-done.4, f32[8,4,4,2]{0,2,3,1:T(4,128)S(1)} %copy.371), channel_id=1, replica_groups=mesh['gx'=16,'gy'=32] {'gx'}, use_global_device_ids=true, to_apply=%region_8.10 | all-reduce | flops 33024 | bytes 198656 | tf_op jit(solution)/shard_map/psum | solution.py:114
  305.4 3.8 all-to-all-start.2
  310.0 120.2 %all-reduce.15.cloned.1.call-done = (f32[8,4,4,2,256]{4,3,2,1,0:T(2,128)}, f32[256,4,32]{0,2,1:T(8,128)}) async-done(((f32[8,4,4,2,256]{4,3,2,1,0:T(2,128)}, f32[256,4,32]{0,2,1:T(8,128)}), (f32[8,4,4,2,256]{4,3,2,1,0:T(2,128)}, f32[256,4,32]{0,2,1:T(8,128)})) %all-reduce.15.cloned.1.call-update) | async-done | bytes 393232 | tf_op jit(solution)/shard_map/psum | solution.py:179
  430.2 1.1 copy.361
  431.3 1.0 reshape.617
  432.3 9.9 %all-to-all-start.1 = ((f32[32,1,1024]{2,1,0:T(1,128)}), f32[32,1,1024]{2,1,0:T(1,128)S(1)}, u32[]{:S(2)}, u32[]{:S(2)}) async-start(f32[32,1,1024]{2,1,0:T(1,128)} %reshape.617), calls=%async_computation.1 | async-start | bytes 262144 | tf_op jit(solution)/shard_map/all_to_all | solution.py:119
  443.1 1.0 gather_fusion.1
  444.1 7.4 all-to-all-done.1
  451.6 1.0 reduce.6
  453.2 1.0 gather_fusion
  455.6 1.3 copy.398
  456.9 2.3 reshape.619
  459.2 12.7 %all_to_all.44 = bf16[32,2,1024]{2,1,0:T(2,128)(2,1)S(1)} all-to-all(bf16[32,2,1024]{2,1,0:T(2,128)(2,1)S(1)} %reshape.619), channel_id=1, replica_groups=mesh['gx'=16,'gy'=32] {'gy'}, dimensions={0} | all-to-all | bytes 262144 | tf_op jit(solution)/shard_map/all_to_all | solution.py:189
  471.9 2.4 reshape.620
  474.4 2.1 copy.400
  476.5 1.3 fusion.16
  477.9 37.7 %all_gather.9 = bf16[256,4,144]{2,1,0:T(4,128)(2,1)S(1)} all-gather(bf16[8,4,144]{2,1,0:T(4,128)(2,1)S(1)} %copy-done.5), channel_id=1, replica_groups=mesh['gx'=16,'gy'=32] {'gy'}, dimensions={0}, use_global_device_ids=true | all-gather | bytes 304128 | tf_op jit(solution)/shard_map/all_gather | solution.py:195
  515.5 115.8 %all-reduce.11.cloned.1.call-done = f32[256,4,144]{2,0,1:T(8,128)} async-done(((f32[256,4,144]{2,0,1:T(8,128)}), f32[256,4,144]{2,0,1:T(8,128)}) %all-reduce.11.cloned.1.call-update) | async-done | bytes 589840 | tf_op jit(solution)/shard_map/psum | solution.py:194
  631.3 1.4 multiply_reduce_fusion.1
  632.8 28.1 %psum.77 = f32[256,4]{0,1:T(4,128)S(1)} all-reduce(f32[256,4]{0,1:T(4,128)S(1)} %multiply_reduce_fusion.1), channel_id=1, replica_groups=mesh['gx'=16,'gy'=32] {'gx'}, use_global_device_ids=true, to_apply=%region_15.17 | all-reduce | flops 1024 | bytes 8192 | tf_op jit(solution)/shard_map/psum | solution.py:196
  660.9 1.6 multiply_reduce_fusion
  662.5 23.6 %psum.78 = f32[256,4]{0,1:T(4,128)S(1)} all-reduce(f32[256,4]{0,1:T(4,128)S(1)} %get-tuple-element.12), channel_id=1, replica_groups=mesh['gx'=16,'gy'=32] {'gx'}, use_global_device_ids=true, to_apply=%region_17.19 | all-reduce | flops 1024 | bytes 8192 | tf_op jit(solution)/shard_map/psum | solution.py:200
  687.8 1.6 pad_maximum_fusion
  689.4 2.1 copy.380
  691.5 1.9 reshape.524
  693.4 3.4 copy.381
  696.9 57.8 %reduce-scatter.2.cloned.1.call-done = f32[16,4,576]{2,0,1:T(8,128)} async-done(((f32[256,4,576]{2,0,1:T(8,128)}), f32[16,4,576]{2,0,1:T(8,128)}) %reduce-scatter.2.cloned.1.call-update) | async-done | bytes 147472 | tf_op jit(solution)/shard_map/reduce_scatter | solution.py:216
  754.7 1.1 fusion.31
  755.8 19.0 %all_gather.11 = bf16[256,4,288]{2,0,1:T(8,128)(2,1)S(1)} all-gather(bf16[16,4,288]{2,0,1:T(8,128)(2,1)S(1)} %fusion.31), channel_id=1, replica_groups=mesh['gx'=16,'gy'=32] {'gx'}, dimensions={0}, use_global_device_ids=true | all-gather | bytes 626688 | tf_op jit(solution)/shard_map/all_gather | solution.py:226
  775.2 1.7 copy.382
  776.9 1.3 dynamic-slice
  778.8 153.4 %all-reduce.13.cloned.1.call-done = f32[256,4,144]{2,1,0:T(4,128)} async-done(((f32[256,4,144]{2,1,0:T(4,128)}), f32[256,4,144]{2,1,0:T(4,128)}) %all-reduce.13.cloned.1.call-update) | async-done | bytes 589840
  933.2 28.1 %psum.79 = f32[8,4]{0,1:T(4,128)S(1)} all-reduce(f32[8,4]{0,1:T(4,128)S(1)} %copy.383), channel_id=1, replica_groups=mesh['gx'=16,'gy'=32] {'gx'}, use_global_device_ids=true, to_apply=%region_21.23 | all-reduce | flops 32 | bytes 256 | tf_op jit(solution)/shard_map/psum | solution.py:231
  (197 shorter events, 30.8 us)
Async XLA Ops:
  6.5 680.5 %copy-start = (bf16[144,288]{1,0:T(8,128)(2,1)S(1)}, bf16[144,288]{1,0:T(8,128)(2,1)}, u32[]{:S(2)}) copy-start(bf16[144,288]{1,0:T(8,128)(2,1)} %param.25) | copy-start | bytes 248836
  6.5 189.6 %all-reduce.9.cloned.1.call-start = ((), (), s32[]{:S(2)}) async-start(), calls=%async_computation.5 | async-start | bytes 524288 | tf_op jit(solution)/shard_map/psum | solution.py:114
  80.2 2.8 copy-start.22
  83.0 4.9 copy-start.14
  85.5 114.1 %copy-start.20 = (s32[8]{0:T(128)}, s32[8]{0:T(128)S(1)}, u32[]{:S(2)}) copy-start(s32[8]{0:T(128)S(1)} %get-tuple-element.15) | copy-start | bytes 100
  196.2 12.1 %copy-start.1 = (f32[256,4,64]{0,2,1:T(8,128)S(1)}, f32[256,4,64]{0,2,1:T(8,128)}, u32[]{:S(2)}) copy-start(f32[256,4,64]{0,2,1:T(8,128)} %all-reduce.9.cloned.1.call-done) | copy-start | bytes 786436
  210.1 15.5 %copy-start.11 = (f32[1,8,4,64]{3,1,2,0:T(8,128)S(1)}, f32[1,8,4,64]{3,1,2,0:T(8,128)}, u32[]{:S(2)}) copy-start(f32[1,8,4,64]{3,1,2,0:T(8,128)} %copy.323) | copy-start | bytes 24580
  210.1 15.5 %copy-start.12 = (f32[1,8,4,64]{3,1,2,0:T(8,128)S(1)}, f32[1,8,4,64]{3,1,2,0:T(8,128)}, u32[]{:S(2)}) copy-start(f32[1,8,4,64]{3,1,2,0:T(8,128)} %copy.324) | copy-start | bytes 24580
  210.1 15.6 %copy-start.10 = (f32[1,8,4,64]{3,1,2,0:T(8,128)S(1)}, f32[1,8,4,64]{3,1,2,0:T(8,128)}, u32[]{:S(2)}) copy-start(f32[1,8,4,64]{3,1,2,0:T(8,128)} %copy.325) | copy-start | bytes 24580
  210.1 15.6 %copy-start.9 = (f32[1,8,4,64]{3,1,2,0:T(8,128)S(1)}, f32[1,8,4,64]{3,1,2,0:T(8,128)}, u32[]{:S(2)}) copy-start(f32[1,8,4,64]{3,1,2,0:T(8,128)} %copy.326) | copy-start | bytes 24580
  210.1 15.6 %copy-start.8 = (f32[1,8,4,64]{3,1,2,0:T(8,128)S(1)}, f32[1,8,4,64]{3,1,2,0:T(8,128)}, u32[]{:S(2)}) copy-start(f32[1,8,4,64]{3,1,2,0:T(8,128)} %copy.327) | copy-start | bytes 24580
  230.6 21.1 %all-to-all-start = ((f32[32,1,2048]{2,1,0:T(1,128)}), f32[32,1,2048]{2,1,0:T(1,128)S(1)}, u32[]{:S(2)}, u32[]{:S(2)}) async-start(f32[32,1,2048]{2,1,0:T(1,128)} %reshape.613), calls=%async_computation | async-start | bytes 524288 | tf_op jit(solution)/shard_map/all_to_all | solution.py:89
  241.2 2.9 copy-start.18
  241.2 3.1 copy-start.15
  253.7 1.2 copy-start.3
  253.7 1.2 copy-start.19
  255.0 2.0 copy-start.4
  256.0 186.5 %copy-start.21 = (s32[8]{0:T(128)S(1)}, s32[8]{0:T(128)}, u32[]{:S(2)}) copy-start(s32[8]{0:T(128)} %copy-done.20) | copy-start | bytes 100
  256.0 186.5 %copy-start.23 = (s32[1,8]{1,0:T(1,128)S(1)}, s32[1,8]{1,0:T(1,128)}, u32[]{:S(2)}) copy-start(s32[1,8]{1,0:T(1,128)} %get-tuple-element.69) | copy-start | bytes 100
  256.0 186.5 %copy-start.24 = (s32[1,8]{1,0:T(1,128)S(1)}, s32[1,8]{1,0:T(1,128)}, u32[]{:S(2)}) copy-start(s32[1,8]{1,0:T(1,128)} %get-tuple-element.67) | copy-start | bytes 100
  256.0 186.5 %copy-start.25 = (s32[1,8]{1,0:T(1,128)S(1)}, s32[1,8]{1,0:T(1,128)}, u32[]{:S(2)}) copy-start(s32[1,8]{1,0:T(1,128)} %fusion.59) | copy-start | bytes 100
  256.0 186.5 %copy-start.26 = (s32[1,8]{1,0:T(1,128)S(1)}, s32[1,8]{1,0:T(1,128)}, u32[]{:S(2)}) copy-start(s32[1,8]{1,0:T(1,128)} %fusion.58) | copy-start | bytes 100
  305.4 126.9 %all-to-all-start.2 = ((bf16[32,2,512]{2,1,0:T(2,128)(2,1)}), bf16[32,2,512]{2,1,0:T(2,128)(2,1)S(1)}, u32[]{:S(2)}, u32[]{:S(2)}) async-start(bf16[32,2,512]{2,1,0:T(2,128)(2,1)} %reshape.615), calls=%async_computation.2 | async-start | bytes 131072 | tf_op jit(solution)/shard_map/all_to_all | solution.py:120
  309.2 120.9 %all-reduce.15.cloned.1.call-start = ((), (), s32[]{:S(2)}) async-start(), calls=%async_computation.9 | async-start | bytes 786432 | tf_op jit(solution)/shard_map/psum | solution.py:179
  432.3 19.3 %all-to-all-start.1 = ((f32[32,1,1024]{2,1,0:T(1,128)}), f32[32,1,1024]{2,1,0:T(1,128)S(1)}, u32[]{:S(2)}, u32[]{:S(2)}) async-start(f32[32,1,1024]{2,1,0:T(1,128)} %reshape.617), calls=%async_computation.1 | async-start | bytes 262144 | tf_op jit(solution)/shard_map/all_to_all | solution.py:119
  442.2 189.1 %all-reduce.11.cloned.1.call-start = ((), (), s32[]{:S(2)}) async-start(), calls=%async_computation.6 | async-start | bytes 2097152 | tf_op jit(solution)/shard_map/psum | solution.py:194
  453.2 2.0 copy-start.27
  471.9 4.6 copy-start.13
  474.3 3.5 copy-start.5
  476.5 184.4 %copy-start.16 = (f32[1,144]{1,0:T(1,128)S(1)}, f32[1,144]{1,0:T(1,128)}, u32[]{:S(2)}) copy-start(f32[1,144]{1,0:T(1,128)} %get-tuple-element.56) | copy-start | bytes 1732
  477.8 208.3 %copy-start.17 = (f32[1,144]{1,0:T(1,128)S(1)}, f32[1,144]{1,0:T(1,128)}, u32[]{:S(2)}) copy-start(f32[1,144]{1,0:T(1,128)} %get-tuple-element.55) | copy-start | bytes 1732
  477.8 276.9 %reduce-scatter.2.cloned.1.call-start = ((), (), s32[]{:S(2)}) async-start(), calls=%async_computation.7 | async-start | bytes 2785280 | tf_op jit(solution)/shard_map/reduce_scatter | solution.py:216
  662.5 23.8 %copy-start.2 = (f32[256,4,144]{2,0,1:T(8,128)}, f32[256,4,144]{2,0,1:T(8,128)S(1)}, u32[]{:S(2)}) copy-start(f32[256,4,144]{2,0,1:T(8,128)S(1)} %get-tuple-element.13) | copy-start | bytes 1769476
  686.3 1.1 copy-start.6
  696.8 77.9 %copy-start.7 = (bf16[288,144]{0,1:T(8,128)(2,1)S(1)}, bf16[288,144]{0,1:T(8,128)(2,1)}, u32[]{:S(2)}) copy-start(bf16[288,144]{0,1:T(8,128)(2,1)} %param.27) | copy-start | bytes 248836
  696.9 235.4 %all-reduce.13.cloned.1.call-start = ((), (), s32[]{:S(2)}) async-start(), calls=%async_computation.8 | async-start | bytes 2097152
Sparse Core Ops, SparseCore 0:
  77.2 118.8 all-reduce.8
  312.7 117.4 all-reduce.14
  477.9 153.3 all-reduce.10
  697.0 57.6 reduce-scatter.1
  777.0 155.1 all-reduce.12
